TPU v7x, 32 devices: a whole 2x2x4 slice. The times are simulated.
32 devices in a mesh: section: 2 (over x), expert: 4 (over y, core), dp: 4 (over z).
Axes of the slice: x: 2, y: 2, z: 4, core: 2. Of those that a mesh axis runs over, the one named last changes fastest.
Arguments:
- inputs: bfloat16 [4, 512, 3072], P(None, ('expert', 'dp')), may hold values from -6 to 6
- upstream: bfloat16 [4, 512, 3072], P(None, ('expert', 'dp')), may hold values from -1.5 to 1.5
- route_mask: int32 [2, 4, 512], P('section', None, ('expert', 'dp')), may hold values from 0 to 1, as said below
- route_weights: float32 [2, 4, 512], P('section', None, ('expert', 'dp')), may hold values from 0.2 to 1
- gate_weight: bfloat16 [2, 3072, 8192], P('section', None, ('expert', 'dp')), may hold values from -0.109375 to 0.109375
- up_weight: bfloat16 [2, 3072, 8192], P('section', None, ('expert', 'dp')), may hold values from -0.109375 to 0.109375
- down_weight: bfloat16 [2, 8192, 3072], P('section', ('expert', 'dp')), may hold values from -0.0625 to 0.0625
Outputs:
- gate_grad: bfloat16 [2, 3072, 8192], P('section', None, ('expert', 'dp'))
- up_grad: bfloat16 [2, 3072, 8192], P('section', None, ('expert', 'dp'))
- down_grad: bfloat16 [2, 8192, 3072], P('section', ('expert', 'dp'))
Inputs may be any that keep to these rules, and one draw needn't show every extreme that they name: `route_mask`: in each layer and micro-batch, each aligned block of 32 tokens (the tokens of one device) has at most 8 ones, and some block exactly 8.
All inputs are finite; a program needn't handle non-finite values.
Results may differ from a plain program's by a relative error of at most 0.0095.
Values may be sent and summed in bfloat16 or wider, within the bound.
A program may use at most 128 MiB of HBM per device.

v0:
```python
import jax
import jax.numpy as jnp
from jax import lax
from jax.sharding import PartitionSpec as P

CAP = 8
EPSILON = 1e-05


def shifted(block, axis, distance):
    devices = range(lax.axis_size(axis))
    route = [(i - distance, i) for i in devices if i - distance in devices]
    return lax.ppermute(block, axis, route)


def normalize(layer_input):
    input_f = layer_input.astype(jnp.float32)
    scale = lax.rsqrt(jnp.mean(input_f * input_f, axis=-1, keepdims=True) + EPSILON)
    return (input_f, scale, (input_f * scale).astype(jnp.bfloat16))


def slot_table(mask_row):
    position = jnp.cumsum(mask_row) - 1
    chosen = (mask_row[:, None] == 1) & (
        position[:, None] == jnp.arange(CAP, dtype=jnp.int32)[None, :]
    )
    return chosen.astype(jnp.bfloat16)


def pick_rows(table, values):
    return lax.dot_general(
        table, values, (((0,), (0,)), ((), ())), preferred_element_type=jnp.float32
    ).astype(jnp.bfloat16)


def layer_forward(layer_input, mask_row, weight_row, gate_w, up_w, down_w):
    input_f, scale, normed = normalize(layer_input)
    table = slot_table(mask_row)
    send_rows = pick_rows(table, normed)
    rows = lax.all_gather(send_rows, ("expert", "dp"), axis=0, tiled=True)
    gate_pre = jnp.dot(rows, gate_w, preferred_element_type=jnp.float32)
    up_pre = jnp.dot(rows, up_w, preferred_element_type=jnp.float32)
    hidden = (jax.nn.silu(gate_pre) * up_pre).astype(jnp.bfloat16)
    summed = lax.psum_scatter(
        jnp.dot(hidden, down_w, preferred_element_type=jnp.float32).astype(jnp.bfloat16),
        ("expert", "dp"),
        scatter_dimension=0,
        tiled=True,
    )
    back = jnp.dot(table, summed, preferred_element_type=jnp.float32)
    output = (input_f + weight_row[:, None] * back).astype(jnp.bfloat16)
    return (output, rows)


def layer_backward(layer_input, mask_row, weight_row, gate_w, up_w, down_w, flowing):
    contract_rows = (((1,), (1,)), ((), ()))
    input_f, scale, normed = normalize(layer_input)
    table = slot_table(mask_row)
    flowing_f = flowing.astype(jnp.float32)
    out_grad = (weight_row[:, None] * flowing_f).astype(jnp.bfloat16)
    send_grad = pick_rows(table, out_grad)
    send_rows = pick_rows(table, normed)
    rows, grad_rows = (
        lax.all_gather(send_rows, ("expert", "dp"), axis=0, tiled=True),
        lax.all_gather(send_grad, ("expert", "dp"), axis=0, tiled=True),
    )
    gate_pre = jnp.dot(rows, gate_w, preferred_element_type=jnp.float32)
    up_pre = jnp.dot(rows, up_w, preferred_element_type=jnp.float32)
    sigma = jax.nn.sigmoid(gate_pre)
    silu_val = jax.nn.silu(gate_pre)
    hidden = (silu_val * up_pre).astype(jnp.bfloat16)
    hidden_grad = lax.dot_general(
        grad_rows, down_w, contract_rows, preferred_element_type=jnp.float32
    )
    gate_pre_grad = (hidden_grad * up_pre * sigma * (1.0 + gate_pre * (1.0 - sigma))).astype(
        jnp.bfloat16
    )
    up_pre_grad = (hidden_grad * silu_val).astype(jnp.bfloat16)
    summed = lax.psum_scatter(
        (
            lax.dot_general(
                gate_pre_grad, gate_w, contract_rows, preferred_element_type=jnp.float32
            )
            + lax.dot_general(up_pre_grad, up_w, contract_rows, preferred_element_type=jnp.float32)
        ).astype(jnp.bfloat16),
        ("expert", "dp"),
        scatter_dimension=0,
        tiled=True,
    )
    total = jnp.dot(table, summed, preferred_element_type=jnp.float32)
    inner = jnp.mean(input_f * total, axis=-1, keepdims=True)
    input_grad = (flowing_f + scale * total - input_f * (scale * scale * scale) * inner).astype(
        jnp.bfloat16
    )
    units = jnp.stack([hidden, gate_pre_grad, up_pre_grad])
    return (input_grad, rows, grad_rows, units)


def store_if(store, index, value, valid):
    older = lax.dynamic_index_in_dim(store, index, 0, keepdims=False)
    return store.at[index].set(jnp.where(valid, value, older))


def shards(inputs, upstream, route_mask, route_weights, gate_weight, up_weight, down_weight):
    sections = lax.axis_size("section")
    section = lax.axis_index("section")
    micro_count = inputs.shape[0]
    token_count = inputs.shape[1]
    model_width = inputs.shape[2]
    hidden_width = gate_weight.shape[2]
    group_rows = lax.axis_size(("expert", "dp")) * CAP
    ticks = micro_count + sections - 1
    gate_w = gate_weight[0]
    up_w = up_weight[0]
    down_w = down_weight[0]
    masks = route_mask[0]
    weights = route_weights[0]
    stash_inputs = jnp.zeros((micro_count, token_count, model_width), jnp.bfloat16)
    stash_rows = jnp.zeros((1,), jnp.bfloat16)

    def forward_tick(tick, carry):
        incoming, stash_inputs, stash_rows = carry
        micro_index = tick - section
        valid = (micro_index >= 0) & (micro_index < micro_count)
        clipped = jnp.clip(micro_index, 0, micro_count - 1)
        first_input = lax.dynamic_index_in_dim(inputs, clipped, 0, keepdims=False)
        current = jnp.where(section == 0, first_input, incoming)
        mask_row = lax.dynamic_index_in_dim(masks, clipped, 0, keepdims=False)
        weight_row = lax.dynamic_index_in_dim(weights, clipped, 0, keepdims=False)
        stash_inputs = store_if(stash_inputs, clipped, current, valid)
        output, rows = layer_forward(current, mask_row, weight_row, gate_w, up_w, down_w)
        finished = jnp.where(valid, output, jnp.zeros_like(output))
        incoming = shifted(finished, "section", 1)
        return (incoming, stash_inputs, stash_rows)

    start = jnp.zeros((token_count, model_width), jnp.bfloat16)
    unused, stash_inputs, stash_rows = lax.fori_loop(
        0, ticks, forward_tick, (start, stash_inputs, stash_rows)
    )
    rows_store = jnp.zeros((micro_count, group_rows, model_width), jnp.bfloat16)
    grads_store = jnp.zeros((micro_count, group_rows, model_width), jnp.bfloat16)
    units_store = jnp.zeros((micro_count, 3, group_rows, hidden_width), jnp.bfloat16)

    def backward_tick(tick, carry):
        incoming, rows_store, grads_store, units_store = carry
        micro_index = tick - (sections - 1 - section)
        valid = (micro_index >= 0) & (micro_index < micro_count)
        clipped = jnp.clip(micro_index, 0, micro_count - 1)
        last_grad = lax.dynamic_index_in_dim(upstream, clipped, 0, keepdims=False)
        current = jnp.where(section == sections - 1, last_grad, incoming)
        mask_row = lax.dynamic_index_in_dim(masks, clipped, 0, keepdims=False)
        weight_row = lax.dynamic_index_in_dim(weights, clipped, 0, keepdims=False)
        layer_input = lax.dynamic_index_in_dim(stash_inputs, clipped, 0, keepdims=False)
        input_grad, rows, grad_rows, units = layer_backward(
            layer_input, mask_row, weight_row, gate_w, up_w, down_w, current
        )
        rows_store = store_if(rows_store, clipped, rows, valid)
        grads_store = store_if(grads_store, clipped, grad_rows, valid)
        units_store = store_if(units_store, clipped, units, valid)
        finished = jnp.where(valid, input_grad, jnp.zeros_like(input_grad))
        incoming = shifted(finished, "section", -1)
        return (incoming, rows_store, grads_store, units_store)

    unused, rows_store, grads_store, units_store = lax.fori_loop(
        0, ticks, backward_tick, (start, rows_store, grads_store, units_store)
    )
    all_rows = rows_store.reshape(-1, model_width)
    all_grads = grads_store.reshape(-1, model_width)
    hidden_all = units_store[:, 0].reshape(-1, hidden_width)
    gate_all = units_store[:, 1].reshape(-1, hidden_width)
    up_all = units_store[:, 2].reshape(-1, hidden_width)
    contract_first = (((0,), (0,)), ((), ()))
    gate_grad = lax.dot_general(
        all_rows, gate_all, contract_first, preferred_element_type=jnp.float32
    )
    up_grad = lax.dot_general(all_rows, up_all, contract_first, preferred_element_type=jnp.float32)
    down_grad = lax.dot_general(
        hidden_all, all_grads, contract_first, preferred_element_type=jnp.float32
    )
    return (
        gate_grad.astype(jnp.bfloat16)[None],
        up_grad.astype(jnp.bfloat16)[None],
        down_grad.astype(jnp.bfloat16)[None],
    )


def solution(mesh):
    return jax.shard_map(
        shards,
        mesh=mesh,
        in_specs=(
            P(None, ("expert", "dp"), None),
            P(None, ("expert", "dp"), None),
            P("section", None, ("expert", "dp")),
            P("section", None, ("expert", "dp")),
            P("section", None, ("expert", "dp")),
            P("section", None, ("expert", "dp")),
            P("section", ("expert", "dp"), None),
        ),
        out_specs=(
            P("section", None, ("expert", "dp")),
            P("section", None, ("expert", "dp")),
            P("section", ("expert", "dp"), None),
        ),
        check_vma=False,
    )
```

profile of v0, /device:TPU:0, one launch (start us, length us, event | category | flops | bytes accessed | tf_op | source)
XLA Modules:
  0.0 1395.9 jit_solution(2319598621400494459)
XLA Ops:
  8.2 588.0 %while.42 = (s32[]{:T(128)}, bf16[32,3072]{1,0:T(8,128)(2,1)S(1)}, bf16[4,32,3072]{2,1,0:T(8,128)(2,1)}, s32[]{:T(128)}, pred[]{:T(512)}, /*index=5*/bf16[4,32,3...) while((s32[]{:T(128)}, bf16[32,3072]{1,0:T(8,128)(2,1)S(1)}, ...), condition=%wide.region_5.6_spmd, body=%wide.region_0.5_spmd.sunk | while | flops 1213294720 | bytes 35229956 | solution.py:137
  15.2 41.6 %all_gather.33 = bf16[128,3072]{1,0:T(8,128)(2,1)S(1)} all-gather(bf16[8,3072]{1,0:T(8,128)(2,1)S(1)} %convolution_convert_fusion.11), channel_id=1, replica_groups=mesh['section'=2,'expert'=4,'dp'=4] {'expert','dp'}, dimensions={0}, use_global_device_ids=true | all-gather | bytes 835584 | tf_op jit(solution)/shard_map/while/body/eval_jaxpr/all_gather | solution.py:40
  65.0 54.6 %reduce-scatter.3.cloned.1.call-done = bf16[8,3072]{1,0:T(8,128)(2,1)} async-done(((bf16[128,3072]{1,0:T(8,128)(2,1)}), bf16[8,3072]{1,0:T(8,128)(2,1)}) %reduce-scatter.3.cloned.1.call-update) | async-done | bytes 49168 | tf_op jit(solution)/shard_map/while/body/eval_jaxpr/reduce_scatter | solution.py:44
  134.4 39.9 %all_gather.33 = bf16[128,3072]{1,0:T(8,128)(2,1)S(1)} all-gather(bf16[8,3072]{1,0:T(8,128)(2,1)S(1)} %convolution_convert_fusion.11), channel_id=1, replica_groups=mesh['section'=2,'expert'=4,'dp'=4] {'expert','dp'}, dimensions={0}, use_global_device_ids=true | all-gather | bytes 835584 | tf_op jit(solution)/shard_map/while/body/eval_jaxpr/all_gather | solution.py:40
  182.6 54.2 %reduce-scatter.3.cloned.1.call-done = bf16[8,3072]{1,0:T(8,128)(2,1)} async-done(((bf16[128,3072]{1,0:T(8,128)(2,1)}), bf16[8,3072]{1,0:T(8,128)(2,1)}) %reduce-scatter.3.cloned.1.call-update) | async-done | bytes 49168 | tf_op jit(solution)/shard_map/while/body/eval_jaxpr/reduce_scatter | solution.py:44
  251.6 39.8 %all_gather.33 = bf16[128,3072]{1,0:T(8,128)(2,1)S(1)} all-gather(bf16[8,3072]{1,0:T(8,128)(2,1)S(1)} %convolution_convert_fusion.11), channel_id=1, replica_groups=mesh['section'=2,'expert'=4,'dp'=4] {'expert','dp'}, dimensions={0}, use_global_device_ids=true | all-gather | bytes 835584 | tf_op jit(solution)/shard_map/while/body/eval_jaxpr/all_gather | solution.py:40
  299.6 54.2 %reduce-scatter.3.cloned.1.call-done = bf16[8,3072]{1,0:T(8,128)(2,1)} async-done(((bf16[128,3072]{1,0:T(8,128)(2,1)}), bf16[8,3072]{1,0:T(8,128)(2,1)}) %reduce-scatter.3.cloned.1.call-update) | async-done | bytes 49168 | tf_op jit(solution)/shard_map/while/body/eval_jaxpr/reduce_scatter | solution.py:44
  368.7 40.0 %all_gather.33 = bf16[128,3072]{1,0:T(8,128)(2,1)S(1)} all-gather(bf16[8,3072]{1,0:T(8,128)(2,1)S(1)} %convolution_convert_fusion.11), channel_id=1, replica_groups=mesh['section'=2,'expert'=4,'dp'=4] {'expert','dp'}, dimensions={0}, use_global_device_ids=true | all-gather | bytes 835584 | tf_op jit(solution)/shard_map/while/body/eval_jaxpr/all_gather | solution.py:40
  416.9 54.2 %reduce-scatter.3.cloned.1.call-done = bf16[8,3072]{1,0:T(8,128)(2,1)} async-done(((bf16[128,3072]{1,0:T(8,128)(2,1)}), bf16[8,3072]{1,0:T(8,128)(2,1)}) %reduce-scatter.3.cloned.1.call-update) | async-done | bytes 49168 | tf_op jit(solution)/shard_map/while/body/eval_jaxpr/reduce_scatter | solution.py:44
  486.0 40.0 %all_gather.33 = bf16[128,3072]{1,0:T(8,128)(2,1)S(1)} all-gather(bf16[8,3072]{1,0:T(8,128)(2,1)S(1)} %convolution_convert_fusion.11), channel_id=1, replica_groups=mesh['section'=2,'expert'=4,'dp'=4] {'expert','dp'}, dimensions={0}, use_global_device_ids=true | all-gather | bytes 835584 | tf_op jit(solution)/shard_map/while/body/eval_jaxpr/all_gather | solution.py:40
  534.2 54.2 %reduce-scatter.3.cloned.1.call-done = bf16[8,3072]{1,0:T(8,128)(2,1)} async-done(((bf16[128,3072]{1,0:T(8,128)(2,1)}), bf16[8,3072]{1,0:T(8,128)(2,1)}) %reduce-scatter.3.cloned.1.call-update) | async-done | bytes 49168 | tf_op jit(solution)/shard_map/while/body/eval_jaxpr/reduce_scatter | solution.py:44
  602.2 772.7 %while.43 = (s32[]{:T(128)}, bf16[32,3072]{1,0:T(8,128)(2,1)}, bf16[4,128,3072]{2,1,0:T(8,128)(2,1)}, bf16[4,128,3072]{2,1,0:T(8,128)(2,1)}, bf16[4,3,128,512]{3...) while((s32[]{:T(128)}, bf16[32,3072]{1,0:T(8,128)(2,1)}, ...), condition=%wide.region_13.14_spmd, body=%wide.region_6.13_spmd.sunk | while | flops 2025212544 | bytes 78193088 | solution.py:164
  607.5 40.1 %all_gather.34 = bf16[128,3072]{1,0:T(8,128)(2,1)S(1)} all-gather(bf16[8,3072]{1,0:T(8,128)(2,1)S(1)} %convolution_convert_fusion.13), channel_id=1, replica_groups=mesh['section'=2,'expert'=4,'dp'=4] {'expert','dp'}, dimensions={0}, use_global_device_ids=true | all-gather | bytes 835584 | tf_op jit(solution)/shard_map/while/body/eval_jaxpr/all_gather | solution.py:64
  696.4 51.1 %reduce-scatter.5.cloned.1.call-done = bf16[8,3072]{1,0:T(8,128)(2,1)} async-done(((bf16[128,3072]{1,0:T(8,128)(2,1)}), bf16[8,3072]{1,0:T(8,128)(2,1)}) %reduce-scatter.5.cloned.1.call-update) | async-done | bytes 49168 | tf_op jit(solution)/shard_map/while/body/eval_jaxpr/reduce_scatter | solution.py:79
  763.0 40.2 %all_gather.34 = bf16[128,3072]{1,0:T(8,128)(2,1)S(1)} all-gather(bf16[8,3072]{1,0:T(8,128)(2,1)S(1)} %convolution_convert_fusion.13), channel_id=1, replica_groups=mesh['section'=2,'expert'=4,'dp'=4] {'expert','dp'}, dimensions={0}, use_global_device_ids=true | all-gather | bytes 835584 | tf_op jit(solution)/shard_map/while/body/eval_jaxpr/all_gather | solution.py:64
  852.1 49.7 %reduce-scatter.5.cloned.1.call-done = bf16[8,3072]{1,0:T(8,128)(2,1)} async-done(((bf16[128,3072]{1,0:T(8,128)(2,1)}), bf16[8,3072]{1,0:T(8,128)(2,1)}) %reduce-scatter.5.cloned.1.call-update) | async-done | bytes 49168 | tf_op jit(solution)/shard_map/while/body/eval_jaxpr/reduce_scatter | solution.py:79
  917.3 39.7 %all_gather.34 = bf16[128,3072]{1,0:T(8,128)(2,1)S(1)} all-gather(bf16[8,3072]{1,0:T(8,128)(2,1)S(1)} %convolution_convert_fusion.13), channel_id=1, replica_groups=mesh['section'=2,'expert'=4,'dp'=4] {'expert','dp'}, dimensions={0}, use_global_device_ids=true | all-gather | bytes 835584 | tf_op jit(solution)/shard_map/while/body/eval_jaxpr/all_gather | solution.py:64
  958.6 35.3 %all_gather.35 = bf16[128,3072]{1,0:T(8,128)(2,1)S(1)} all-gather(bf16[8,3072]{1,0:T(8,128)(2,1)S(1)} %convolution_convert_fusion.14), channel_id=1, replica_groups=mesh['section'=2,'expert'=4,'dp'=4] {'expert','dp'}, dimensions={0}, use_global_device_ids=true | all-gather | bytes 835584 | tf_op jit(solution)/shard_map/while/body/eval_jaxpr/all_gather | solution.py:65
  1006.0 49.7 %reduce-scatter.5.cloned.1.call-done = bf16[8,3072]{1,0:T(8,128)(2,1)} async-done(((bf16[128,3072]{1,0:T(8,128)(2,1)}), bf16[8,3072]{1,0:T(8,128)(2,1)}) %reduce-scatter.5.cloned.1.call-update) | async-done | bytes 49168 | tf_op jit(solution)/shard_map/while/body/eval_jaxpr/reduce_scatter | solution.py:79
  1071.2 40.1 %all_gather.34 = bf16[128,3072]{1,0:T(8,128)(2,1)S(1)} all-gather(bf16[8,3072]{1,0:T(8,128)(2,1)S(1)} %convolution_convert_fusion.13), channel_id=1, replica_groups=mesh['section'=2,'expert'=4,'dp'=4] {'expert','dp'}, dimensions={0}, use_global_device_ids=true | all-gather | bytes 835584 | tf_op jit(solution)/shard_map/while/body/eval_jaxpr/all_gather | solution.py:64
  1112.9 35.3 %all_gather.35 = bf16[128,3072]{1,0:T(8,128)(2,1)S(1)} all-gather(bf16[8,3072]{1,0:T(8,128)(2,1)S(1)} %convolution_convert_fusion.14), channel_id=1, replica_groups=mesh['section'=2,'expert'=4,'dp'=4] {'expert','dp'}, dimensions={0}, use_global_device_ids=true | all-gather | bytes 835584 | tf_op jit(solution)/shard_map/while/body/eval_jaxpr/all_gather | solution.py:65
  1160.3 49.8 %reduce-scatter.5.cloned.1.call-done = bf16[8,3072]{1,0:T(8,128)(2,1)} async-done(((bf16[128,3072]{1,0:T(8,128)(2,1)}), bf16[8,3072]{1,0:T(8,128)(2,1)}) %reduce-scatter.5.cloned.1.call-update) | async-done | bytes 49168 | tf_op jit(solution)/shard_map/while/body/eval_jaxpr/reduce_scatter | solution.py:79
  1225.7 40.2 %all_gather.34 = bf16[128,3072]{1,0:T(8,128)(2,1)S(1)} all-gather(bf16[8,3072]{1,0:T(8,128)(2,1)S(1)} %convolution_convert_fusion.13), channel_id=1, replica_groups=mesh['section'=2,'expert'=4,'dp'=4] {'expert','dp'}, dimensions={0}, use_global_device_ids=true | all-gather | bytes 835584 | tf_op jit(solution)/shard_map/while/body/eval_jaxpr/all_gather | solution.py:64
  1314.8 49.8 %reduce-scatter.5.cloned.1.call-done = bf16[8,3072]{1,0:T(8,128)(2,1)} async-done(((bf16[128,3072]{1,0:T(8,128)(2,1)}), bf16[8,3072]{1,0:T(8,128)(2,1)}) %reduce-scatter.5.cloned.1.call-update) | async-done | bytes 49168 | tf_op jit(solution)/shard_map/while/body/eval_jaxpr/reduce_scatter | solution.py:79
  (344 shorter events, 387.2 us)
Async XLA Ops:
  8.2 111.4 %reduce-scatter.3.cloned.1.call-start = ((), (), s32[]{:S(2)}) async-start(), calls=%async_computation.2 | async-start | bytes 835584 | tf_op jit(solution)/shard_map/while/body/eval_jaxpr/reduce_scatter | solution.py:44
  120.8 6.5 collective-permute-start
  127.4 109.4 %reduce-scatter.3.cloned.1.call-start = ((), (), s32[]{:S(2)}) async-start(), calls=%async_computation.2 | async-start | bytes 835584 | tf_op jit(solution)/shard_map/while/body/eval_jaxpr/reduce_scatter | solution.py:44
  238.0 6.6 collective-permute-start
  244.6 109.3 %reduce-scatter.3.cloned.1.call-start = ((), (), s32[]{:S(2)}) async-start(), calls=%async_computation.2 | async-start | bytes 835584 | tf_op jit(solution)/shard_map/while/body/eval_jaxpr/reduce_scatter | solution.py:44
  355.1 6.5 collective-permute-start
  361.6 109.5 %reduce-scatter.3.cloned.1.call-start = ((), (), s32[]{:S(2)}) async-start(), calls=%async_computation.2 | async-start | bytes 835584 | tf_op jit(solution)/shard_map/while/body/eval_jaxpr/reduce_scatter | solution.py:44
  472.3 6.6 collective-permute-start
  478.9 109.5 %reduce-scatter.3.cloned.1.call-start = ((), (), s32[]{:S(2)}) async-start(), calls=%async_computation.2 | async-start | bytes 835584 | tf_op jit(solution)/shard_map/while/body/eval_jaxpr/reduce_scatter | solution.py:44
  589.6 6.6 collective-permute-start
  602.2 145.3 %reduce-scatter.5.cloned.1.call-start = ((), (), s32[]{:S(2)}) async-start(), calls=%async_computation.3 | async-start | bytes 835584 | tf_op jit(solution)/shard_map/while/body/eval_jaxpr/reduce_scatter | solution.py:79
  607.4 77.5 %copy-start.3 = (bf16[512,3072]{1,0:T(8,128)(2,1)S(1)}, bf16[512,3072]{1,0:T(8,128)(2,1)}, u32[]{:S(2)}) copy-start(bf16[512,3072]{1,0:T(8,128)(2,1)} %get-tuple-element.1002) | copy-start | bytes 9437188 | tf_op jit(solution)/shard_map/while
  750.1 7.7 collective-permute-start.1
  757.8 144.0 %reduce-scatter.5.cloned.1.call-start = ((), (), s32[]{:S(2)}) async-start(), calls=%async_computation.3 | async-start | bytes 835584 | tf_op jit(solution)/shard_map/while/body/eval_jaxpr/reduce_scatter | solution.py:79
  763.0 77.6 %copy-start.3 = (bf16[512,3072]{1,0:T(8,128)(2,1)S(1)}, bf16[512,3072]{1,0:T(8,128)(2,1)}, u32[]{:S(2)}) copy-start(bf16[512,3072]{1,0:T(8,128)(2,1)} %get-tuple-element.1002) | copy-start | bytes 9437188 | tf_op jit(solution)/shard_map/while
  904.4 7.7 collective-permute-start.1
  912.1 143.6 %reduce-scatter.5.cloned.1.call-start = ((), (), s32[]{:S(2)}) async-start(), calls=%async_computation.3 | async-start | bytes 835584 | tf_op jit(solution)/shard_map/while/body/eval_jaxpr/reduce_scatter | solution.py:79
  1058.4 7.7 collective-permute-start.1
  1066.0 144.1 %reduce-scatter.5.cloned.1.call-start = ((), (), s32[]{:S(2)}) async-start(), calls=%async_computation.3 | async-start | bytes 835584 | tf_op jit(solution)/shard_map/while/body/eval_jaxpr/reduce_scatter | solution.py:79
  1071.2 77.6 %copy-start.3 = (bf16[512,3072]{1,0:T(8,128)(2,1)S(1)}, bf16[512,3072]{1,0:T(8,128)(2,1)}, u32[]{:S(2)}) copy-start(bf16[512,3072]{1,0:T(8,128)(2,1)} %get-tuple-element.1002) | copy-start | bytes 9437188 | tf_op jit(solution)/shard_map/while
  1212.8 7.7 collective-permute-start.1
  1220.5 144.2 %reduce-scatter.5.cloned.1.call-start = ((), (), s32[]{:S(2)}) async-start(), calls=%async_computation.3 | async-start | bytes 835584 | tf_op jit(solution)/shard_map/while/body/eval_jaxpr/reduce_scatter | solution.py:79
  1225.7 77.7 %copy-start.3 = (bf16[512,3072]{1,0:T(8,128)(2,1)S(1)}, bf16[512,3072]{1,0:T(8,128)(2,1)}, u32[]{:S(2)}) copy-start(bf16[512,3072]{1,0:T(8,128)(2,1)} %get-tuple-element.1002) | copy-start | bytes 9437188 | tf_op jit(solution)/shard_map/while
  1367.3 7.7 collective-permute-start.1
  (44 other events, 775.8 us)
Sparse Core Ops, SparseCore 0:
  64.5 55.1 reduce-scatter.2
  182.0 54.7 reduce-scatter.2
  299.1 54.7 reduce-scatter.2
  416.4 54.7 reduce-scatter.2
  533.6 54.7 reduce-scatter.2
  690.9 56.5 reduce-scatter.4
  846.5 55.2 reduce-scatter.4
  1000.4 55.2 reduce-scatter.4
  1154.8 55.3 reduce-scatter.4
  1309.3 55.3 reduce-scatter.4
where the time goes:
time: 1400 us
  blocking collectives  578 us (41%)
  waiting for transfers between devices  550 us (39%)
  matrix products  102 us (7%)
  other arithmetic  84.4 us (6%)
  local copies, waits for them, and re-layouts  43.7 us (3%)
  starting transfers between devices  23.4 us (2%)
  between operations  14 us (1%)
    reduce_scatter x5, waiting for transfers between devices, layer_forward(): lax.psum_scatter(jnp.dot(hidden, down_w, preferred_element_type=jnp.float...  271 us
    reduce_scatter x5, waiting for transfers between devices, layer_backward(): lax.psum_scatter((lax.dot_general(gate_pre_grad, gate_w, contract_rows, p...  250 us
    all_gather x5, blocking collectives, layer_forward(): rows = lax.all_gather(send_rows, ('expert', 'dp'), axis=0, tiled=True)  201 us
    all_gather x5, blocking collectives, layer_backward(): lax.all_gather(send_rows, ('expert', 'dp'), axis=0, tiled=True)  200 us
    all_gather x5, blocking collectives, layer_backward(): lax.all_gather(send_grad, ('expert', 'dp'), axis=0, tiled=True)  176 us
    scatter x20, other arithmetic, store_if(): return store.at[index].set(jnp.where(valid, value, older))  42.4 us
  transfers between devices with their start and end apart: 20, of which 20 were waited for; matrix products, arithmetic and copies ran while one was open for 4% of the time, Pallas kernels for 0%

commit v1 on v0

--- a/solution.py
+++ b/solution.py
@@ -37,7 +37,27 @@
     input_f, scale, normed = normalize(layer_input)
     table = slot_table(mask_row)
     send_rows = pick_rows(table, normed)
-    rows = lax.all_gather(send_rows, ("expert", "dp"), axis=0, tiled=True)
+    size, mine, span = (
+        lax.axis_size(("expert", "dp")),
+        lax.axis_index(("expert", "dp")),
+        send_rows.shape[0],
+    )
+    ahead = [(i_2, (i_2 + 1) % size) for i_2 in range(size)]
+    left = [(i_2, (i_2 - 1) % size) for i_2 in range(size)]
+    rows = jnp.zeros(
+        (*send_rows.shape[:0], size * span, *send_rows.shape[0 + 1 :]), send_rows.dtype
+    )
+    rows = lax.dynamic_update_slice_in_dim(rows, send_rows, mine * span, axis=0)
+    from_left = from_right = send_rows
+    half = size // 2
+    for step in range(1, half + 1):
+        from_left = lax.ppermute(from_left, ("expert", "dp"), ahead)
+        rows = lax.dynamic_update_slice_in_dim(rows, from_left, (mine - step) % size * span, axis=0)
+        if step < size - half:
+            from_right = lax.ppermute(from_right, ("expert", "dp"), left)
+            rows = lax.dynamic_update_slice_in_dim(
+                rows, from_right, (mine + step) % size * span, axis=0
+            )
     gate_pre = jnp.dot(rows, gate_w, preferred_element_type=jnp.float32)
     up_pre = jnp.dot(rows, up_w, preferred_element_type=jnp.float32)
     hidden = (jax.nn.silu(gate_pre) * up_pre).astype(jnp.bfloat16)

time: 1400 us -> 1460 us (1.043)
  blocking collectives: 578 us -> 377 us
  starting transfers between devices: 23.4 us -> 162 us
  waiting for transfers between devices: 550 us -> 632 us
  local copies, waits for them, and re-layouts: 43.7 us -> 87.6 us
    all_gather x5 -> x0, blocking collectives: 201 us -> none  [layer_forward(): rows = lax.all_gather(send_rows, ('expert', 'dp'), axis=0, tiled=True)]
    ppermute x0 -> x75, starting transfers between devices: none -> 139 us  [the longest x35 129 us: layer_forward(): from_right = lax.ppermute(from_right, ('expert', 'dp'), left)]
    ppermute x0 -> x75, waiting for transfers between devices: none -> 79.1 us  [the longest x40 58.4 us: layer_forward(): from_left = lax.ppermute(from_left, ('expert', 'dp'), ahead)]
    dynamic_update_slice x0 -> x75, local copies, waits for them, and re-layouts: none -> 46.7 us  [the longest x40 24.9 us: layer_forward(): lax.dynamic_update_slice_in_dim(rows, from_left, (mine - step) % size * s...]
  transfers between devices with their start and end apart: 20 -> 95, of which waited for: 20 -> 74; matrix products, arithmetic and copies ran while one was open for 4% -> 6% of each run, Pallas kernels for 0% -> 0%
where the time goes in v1:
time: 1460 us
  waiting for transfers between devices  632 us (43%)
  blocking collectives  377 us (26%)
  starting transfers between devices  162 us (11%)
  matrix products  113 us (8%)
  local copies, waits for them, and re-layouts  87.6 us (6%)
  other arithmetic  74.2 us (5%)
    reduce_scatter x5, waiting for transfers between devices, layer_forward(): lax.psum_scatter(jnp.dot(hidden, down_w, preferred_element_type=jnp.float...  273 us
    reduce_scatter x5, waiting for transfers between devices, layer_backward(): lax.psum_scatter((lax.dot_general(gate_pre_grad, gate_w, contract_rows, p...  249 us
    all_gather x5, blocking collectives, layer_backward(): lax.all_gather(send_rows, ('expert', 'dp'), axis=0, tiled=True)  200 us
    all_gather x5, blocking collectives, layer_backward(): lax.all_gather(send_grad, ('expert', 'dp'), axis=0, tiled=True)  177 us
    ppermute x35, starting transfers between devices, layer_forward(): from_right = lax.ppermute(from_right, ('expert', 'dp'), left)  129 us
    ppermute x40, waiting for transfers between devices, layer_forward(): from_left = lax.ppermute(from_left, ('expert', 'dp'), ahead)  58.4 us
    scatter x20, other arithmetic, store_if(): return store.at[index].set(jnp.where(valid, value, older))  41.6 us
    ppermute x10, waiting for transfers between devices, shifted(): return lax.ppermute(block, axis, route)  31.2 us
  transfers between devices with their start and end apart: 95, of which 74 were waited for; matrix products, arithmetic and copies ran while one was open for 6% of the time, Pallas kernels for 0%

profile of v1, /device:TPU:0, one launch (start us, length us, event | category | flops | bytes accessed | tf_op | source)
XLA Modules:
  0.0 1460.9 jit_solution(14714098769517229894)
XLA Ops:
  8.2 659.4 %while.43 = (s32[]{:T(128)}, bf16[32,3072]{1,0:T(8,128)(2,1)S(1)}, bf16[4,32,3072]{2,1,0:T(8,128)(2,1)}, s32[]{:T(128)}, pred[]{:T(512)}, /*index=5*/bf16[4,32,3...) while((s32[]{:T(128)}, bf16[32,3072]{1,0:T(8,128)(2,1)S(1)}, ...), condition=%wide.region_5.6_spmd, body=%wide.region_0.5_spmd.sunk | while | flops 1213294976 | bytes 35724864 | solution.py:157
  16.5 5.4 collective-permute-start.1
  82.4 53.3 %reduce-scatter.3.cloned.1.call-done = bf16[8,3072]{1,0:T(8,128)(2,1)} async-done(((bf16[128,3072]{1,0:T(8,128)(2,1)}), bf16[8,3072]{1,0:T(8,128)(2,1)}) %reduce-scatter.3.cloned.1.call-update) | async-done | bytes 49168 | tf_op jit(solution)/shard_map/while/body/eval_jaxpr/reduce_scatter | solution.py:64
  211.8 54.9 %reduce-scatter.3.cloned.1.call-done = bf16[8,3072]{1,0:T(8,128)(2,1)} async-done(((bf16[128,3072]{1,0:T(8,128)(2,1)}), bf16[8,3072]{1,0:T(8,128)(2,1)}) %reduce-scatter.3.cloned.1.call-update) | async-done | bytes 49168 | tf_op jit(solution)/shard_map/while/body/eval_jaxpr/reduce_scatter | solution.py:64
  342.9 54.9 %reduce-scatter.3.cloned.1.call-done = bf16[8,3072]{1,0:T(8,128)(2,1)} async-done(((bf16[128,3072]{1,0:T(8,128)(2,1)}), bf16[8,3072]{1,0:T(8,128)(2,1)}) %reduce-scatter.3.cloned.1.call-update) | async-done | bytes 49168 | tf_op jit(solution)/shard_map/while/body/eval_jaxpr/reduce_scatter | solution.py:64
  473.8 55.0 %reduce-scatter.3.cloned.1.call-done = bf16[8,3072]{1,0:T(8,128)(2,1)} async-done(((bf16[128,3072]{1,0:T(8,128)(2,1)}), bf16[8,3072]{1,0:T(8,128)(2,1)}) %reduce-scatter.3.cloned.1.call-update) | async-done | bytes 49168 | tf_op jit(solution)/shard_map/while/body/eval_jaxpr/reduce_scatter | solution.py:64
  605.1 54.8 %reduce-scatter.3.cloned.1.call-done = bf16[8,3072]{1,0:T(8,128)(2,1)} async-done(((bf16[128,3072]{1,0:T(8,128)(2,1)}), bf16[8,3072]{1,0:T(8,128)(2,1)}) %reduce-scatter.3.cloned.1.call-update) | async-done | bytes 49168 | tf_op jit(solution)/shard_map/while/body/eval_jaxpr/reduce_scatter | solution.py:64
  673.6 766.3 %while.44 = (s32[]{:T(128)}, bf16[32,3072]{1,0:T(8,128)(2,1)}, bf16[4,128,3072]{2,1,0:T(8,128)(2,1)}, bf16[4,128,3072]{2,1,0:T(8,128)(2,1)}, bf16[4,3,128,512]{3...) while((s32[]{:T(128)}, bf16[32,3072]{1,0:T(8,128)(2,1)}, ...), condition=%wide.region_13.14_spmd, body=%wide.region_6.13_spmd.sunk | while | flops 2025212544 | bytes 78193088 | solution.py:184
  677.0 40.1 %all_gather.22 = bf16[128,3072]{1,0:T(8,128)(2,1)S(1)} all-gather(bf16[8,3072]{1,0:T(8,128)(2,1)S(1)} %convolution_convert_fusion.11), channel_id=1, replica_groups=mesh['section'=2,'expert'=4,'dp'=4] {'expert','dp'}, dimensions={0}, use_global_device_ids=true | all-gather | bytes 835584 | tf_op jit(solution)/shard_map/while/body/eval_jaxpr/all_gather | solution.py:84
  718.7 35.1 %all_gather.23 = bf16[128,3072]{1,0:T(8,128)(2,1)S(1)} all-gather(bf16[8,3072]{1,0:T(8,128)(2,1)S(1)} %convolution_convert_fusion.12), channel_id=1, replica_groups=mesh['section'=2,'expert'=4,'dp'=4] {'expert','dp'}, dimensions={0}, use_global_device_ids=true | all-gather | bytes 835584 | tf_op jit(solution)/shard_map/while/body/eval_jaxpr/all_gather | solution.py:85
  766.7 51.2 %reduce-scatter.5.cloned.1.call-done = bf16[8,3072]{1,0:T(8,128)(2,1)} async-done(((bf16[128,3072]{1,0:T(8,128)(2,1)}), bf16[8,3072]{1,0:T(8,128)(2,1)}) %reduce-scatter.5.cloned.1.call-update) | async-done | bytes 49168 | tf_op jit(solution)/shard_map/while/body/eval_jaxpr/reduce_scatter | solution.py:99
  831.5 40.2 %all_gather.22 = bf16[128,3072]{1,0:T(8,128)(2,1)S(1)} all-gather(bf16[8,3072]{1,0:T(8,128)(2,1)S(1)} %convolution_convert_fusion.11), channel_id=1, replica_groups=mesh['section'=2,'expert'=4,'dp'=4] {'expert','dp'}, dimensions={0}, use_global_device_ids=true | all-gather | bytes 835584 | tf_op jit(solution)/shard_map/while/body/eval_jaxpr/all_gather | solution.py:84
  873.3 35.4 %all_gather.23 = bf16[128,3072]{1,0:T(8,128)(2,1)S(1)} all-gather(bf16[8,3072]{1,0:T(8,128)(2,1)S(1)} %convolution_convert_fusion.12), channel_id=1, replica_groups=mesh['section'=2,'expert'=4,'dp'=4] {'expert','dp'}, dimensions={0}, use_global_device_ids=true | all-gather | bytes 835584 | tf_op jit(solution)/shard_map/while/body/eval_jaxpr/all_gather | solution.py:85
  921.6 49.4 %reduce-scatter.5.cloned.1.call-done = bf16[8,3072]{1,0:T(8,128)(2,1)} async-done(((bf16[128,3072]{1,0:T(8,128)(2,1)}), bf16[8,3072]{1,0:T(8,128)(2,1)}) %reduce-scatter.5.cloned.1.call-update) | async-done | bytes 49168 | tf_op jit(solution)/shard_map/while/body/eval_jaxpr/reduce_scatter | solution.py:99
  984.6 40.0 %all_gather.22 = bf16[128,3072]{1,0:T(8,128)(2,1)S(1)} all-gather(bf16[8,3072]{1,0:T(8,128)(2,1)S(1)} %convolution_convert_fusion.11), channel_id=1, replica_groups=mesh['section'=2,'expert'=4,'dp'=4] {'expert','dp'}, dimensions={0}, use_global_device_ids=true | all-gather | bytes 835584 | tf_op jit(solution)/shard_map/while/body/eval_jaxpr/all_gather | solution.py:84
  1026.2 35.4 %all_gather.23 = bf16[128,3072]{1,0:T(8,128)(2,1)S(1)} all-gather(bf16[8,3072]{1,0:T(8,128)(2,1)S(1)} %convolution_convert_fusion.12), channel_id=1, replica_groups=mesh['section'=2,'expert'=4,'dp'=4] {'expert','dp'}, dimensions={0}, use_global_device_ids=true | all-gather | bytes 835584 | tf_op jit(solution)/shard_map/while/body/eval_jaxpr/all_gather | solution.py:85
  1074.5 49.3 %reduce-scatter.5.cloned.1.call-done = bf16[8,3072]{1,0:T(8,128)(2,1)} async-done(((bf16[128,3072]{1,0:T(8,128)(2,1)}), bf16[8,3072]{1,0:T(8,128)(2,1)}) %reduce-scatter.5.cloned.1.call-update) | async-done | bytes 49168 | tf_op jit(solution)/shard_map/while/body/eval_jaxpr/reduce_scatter | solution.py:99
  1137.4 39.8 %all_gather.22 = bf16[128,3072]{1,0:T(8,128)(2,1)S(1)} all-gather(bf16[8,3072]{1,0:T(8,128)(2,1)S(1)} %convolution_convert_fusion.11), channel_id=1, replica_groups=mesh['section'=2,'expert'=4,'dp'=4] {'expert','dp'}, dimensions={0}, use_global_device_ids=true | all-gather | bytes 835584 | tf_op jit(solution)/shard_map/while/body/eval_jaxpr/all_gather | solution.py:84
  1178.8 35.3 %all_gather.23 = bf16[128,3072]{1,0:T(8,128)(2,1)S(1)} all-gather(bf16[8,3072]{1,0:T(8,128)(2,1)S(1)} %convolution_convert_fusion.12), channel_id=1, replica_groups=mesh['section'=2,'expert'=4,'dp'=4] {'expert','dp'}, dimensions={0}, use_global_device_ids=true | all-gather | bytes 835584 | tf_op jit(solution)/shard_map/while/body/eval_jaxpr/all_gather | solution.py:85
  1227.0 49.6 %reduce-scatter.5.cloned.1.call-done = bf16[8,3072]{1,0:T(8,128)(2,1)} async-done(((bf16[128,3072]{1,0:T(8,128)(2,1)}), bf16[8,3072]{1,0:T(8,128)(2,1)}) %reduce-scatter.5.cloned.1.call-update) | async-done | bytes 49168 | tf_op jit(solution)/shard_map/while/body/eval_jaxpr/reduce_scatter | solution.py:99
  1290.3 40.1 %all_gather.22 = bf16[128,3072]{1,0:T(8,128)(2,1)S(1)} all-gather(bf16[8,3072]{1,0:T(8,128)(2,1)S(1)} %convolution_convert_fusion.11), channel_id=1, replica_groups=mesh['section'=2,'expert'=4,'dp'=4] {'expert','dp'}, dimensions={0}, use_global_device_ids=true | all-gather | bytes 835584 | tf_op jit(solution)/shard_map/while/body/eval_jaxpr/all_gather | solution.py:84
  1331.9 35.4 %all_gather.23 = bf16[128,3072]{1,0:T(8,128)(2,1)S(1)} all-gather(bf16[8,3072]{1,0:T(8,128)(2,1)S(1)} %convolution_convert_fusion.12), channel_id=1, replica_groups=mesh['section'=2,'expert'=4,'dp'=4] {'expert','dp'}, dimensions={0}, use_global_device_ids=true | all-gather | bytes 835584 | tf_op jit(solution)/shard_map/while/body/eval_jaxpr/all_gather | solution.py:85
  1380.2 49.4 %reduce-scatter.5.cloned.1.call-done = bf16[8,3072]{1,0:T(8,128)(2,1)} async-done(((bf16[128,3072]{1,0:T(8,128)(2,1)}), bf16[8,3072]{1,0:T(8,128)(2,1)}) %reduce-scatter.5.cloned.1.call-update) | async-done | bytes 49168 | tf_op jit(solution)/shard_map/while/body/eval_jaxpr/reduce_scatter | solution.py:99
  1441.4 5.5 fusion.56
  (553 shorter events, 536.1 us)
Async XLA Ops:
  8.2 127.5 %reduce-scatter.3.cloned.1.call-start = ((), (), s32[]{:S(2)}) async-start(), calls=%async_computation.2 | async-start | bytes 835584 | tf_op jit(solution)/shard_map/while/body/eval_jaxpr/reduce_scatter | solution.py:64
  16.5 7.2 collective-permute-start.1
  21.9 6.9 collective-permute-start
  55.9 11.9 collective-permute-start.13
  143.3 123.5 %reduce-scatter.3.cloned.1.call-start = ((), (), s32[]{:S(2)}) async-start(), calls=%async_computation.2 | async-start | bytes 835584 | tf_op jit(solution)/shard_map/while/body/eval_jaxpr/reduce_scatter | solution.py:64
  185.4 11.9 collective-permute-start.13
  274.4 123.4 %reduce-scatter.3.cloned.1.call-start = ((), (), s32[]{:S(2)}) async-start(), calls=%async_computation.2 | async-start | bytes 835584 | tf_op jit(solution)/shard_map/while/body/eval_jaxpr/reduce_scatter | solution.py:64
  308.4 6.7 collective-permute-start.8
  316.4 11.9 collective-permute-start.13
  405.4 123.4 %reduce-scatter.3.cloned.1.call-start = ((), (), s32[]{:S(2)}) async-start(), calls=%async_computation.2 | async-start | bytes 835584 | tf_op jit(solution)/shard_map/while/body/eval_jaxpr/reduce_scatter | solution.py:64
  447.4 11.8 collective-permute-start.13
  536.5 123.4 %reduce-scatter.3.cloned.1.call-start = ((), (), s32[]{:S(2)}) async-start(), calls=%async_computation.2 | async-start | bytes 835584 | tf_op jit(solution)/shard_map/while/body/eval_jaxpr/reduce_scatter | solution.py:64
  570.6 6.8 collective-permute-start.8
  578.6 11.9 collective-permute-start.13
  673.6 144.3 %reduce-scatter.5.cloned.1.call-start = ((), (), s32[]{:S(2)}) async-start(), calls=%async_computation.3 | async-start | bytes 835584 | tf_op jit(solution)/shard_map/while/body/eval_jaxpr/reduce_scatter | solution.py:99
  820.6 7.7 collective-permute-start.16
  828.3 142.8 %reduce-scatter.5.cloned.1.call-start = ((), (), s32[]{:S(2)}) async-start(), calls=%async_computation.3 | async-start | bytes 835584 | tf_op jit(solution)/shard_map/while/body/eval_jaxpr/reduce_scatter | solution.py:99
  973.7 7.7 collective-permute-start.16
  981.3 142.5 %reduce-scatter.5.cloned.1.call-start = ((), (), s32[]{:S(2)}) async-start(), calls=%async_computation.3 | async-start | bytes 835584 | tf_op jit(solution)/shard_map/while/body/eval_jaxpr/reduce_scatter | solution.py:99
  1126.5 7.7 collective-permute-start.16
  1134.1 142.5 %reduce-scatter.5.cloned.1.call-start = ((), (), s32[]{:S(2)}) async-start(), calls=%async_computation.3 | async-start | bytes 835584 | tf_op jit(solution)/shard_map/while/body/eval_jaxpr/reduce_scatter | solution.py:99
  1279.3 7.7 collective-permute-start.16
  1287.0 142.7 %reduce-scatter.5.cloned.1.call-start = ((), (), s32[]{:S(2)}) async-start(), calls=%async_computation.3 | async-start | bytes 835584 | tf_op jit(solution)/shard_map/while/body/eval_jaxpr/reduce_scatter | solution.py:99
  1432.3 7.7 collective-permute-start.16
  (111 other events, 1371.7 us)
Sparse Core Ops, SparseCore 0:
  81.8 53.7 reduce-scatter.2
  211.2 55.4 reduce-scatter.2
  342.3 55.4 reduce-scatter.2
  473.3 55.5 reduce-scatter.2
  604.5 55.3 reduce-scatter.2
  761.0 56.9 reduce-scatter.4
  915.9 55.1 reduce-scatter.4
  1068.7 55.0 reduce-scatter.4
  1221.3 55.3 reduce-scatter.4
  1374.5 55.0 reduce-scatter.4
